TPU v7x, 32 devices: a whole 2x2x4 slice. The times are simulated.
32 devices in a mesh: groups: 2 (over x), tm: 16 (over z, y, core).
Axes of the slice: x: 2, y: 2, z: 4, core: 2. Of those that a mesh axis runs over, the one named last changes fastest.
Arguments:
- token_ids: int32 [4096, 8], P(('groups', 'tm')), parts along dimension 0, may hold values from 0 to 127
- field_offsets: int32 [16], P('groups'), parts along dimension 0, may hold values from 0 to 896
- embed_table: bfloat16 [1024, 1024], replicated, may hold values from -2.09375 to 2.09375
- w_in: bfloat16 [1024, 3072], P('tm'), may hold values from -0.1875 to 0.1875
- short_taps: float32 [3, 3072], replicated, may hold values from -1 to 1
- filters: bfloat16 [2, 1024, 2048], P(None, 'tm'), may hold values from -1.1 to 1.1
- cotangent: bfloat16 [4096, 1024], P(('groups', 'tm')), parts along dimension 0, may hold values from -0.125 to 0.125
Outputs:
- mixer_out: bfloat16 [4096, 1024], P(('groups', 'tm')), parts along dimension 0
- weight_grads: float32 [2048, 3072], P(('groups', 'tm')), parts along dimension 0
- tap_grads: float32 [6, 3072], P('groups'), parts along dimension 0
- filter_grads: float32 [4, 1024, 2048], P('groups', 'tm'), parts along dimension 0
There are 2 independent parts, one for each index of `groups`. A program takes and returns all parts, laid end to end along the dimension named above; an argument that names none is the same for every part. Nothing has to cross between parts.
All inputs are finite; a program needn't handle non-finite values.
Results may differ from a plain program's by a relative error of at most 0.035.
Values may be sent and summed in bfloat16 or wider, within the bound.
A program may use at most 128 MiB of HBM per device.

v0:
```python
import math
import jax
import jax.numpy as jnp
from jax import lax
from jax.sharding import PartitionSpec as P

HIGHEST = lax.Precision.HIGHEST


def shifted(value, axis, steps):
    count = lax.axis_size(axis)
    initial, last = (max(0, -steps), min(count, count - steps))
    return lax.ppermute(value, axis, [(source, source + steps) for source in range(initial, last)])


def cis_tables(count_a, count_b, modulus):
    left = jnp.arange(count_a, dtype=jnp.int32)[:, None]
    right = jnp.arange(count_b, dtype=jnp.int32)[None, :]
    angle = 2.0 * math.pi / modulus * (left * right % modulus).astype(jnp.float32)
    return (jnp.cos(angle), jnp.sin(angle))


def build_tables(first_len, second_len, total):
    first_cos, first_sin = cis_tables(first_len, first_len // 2, first_len)
    twist_cos, twist_sin = cis_tables(first_len, second_len, total)
    second_cos, second_sin = cis_tables(second_len, second_len, second_len)
    first_both = jnp.concatenate([first_cos, -first_sin], axis=0)
    forward_second = jnp.concatenate(
        [
            jnp.concatenate([second_cos, -second_sin], axis=1),
            jnp.concatenate([second_sin, second_cos], axis=1),
        ],
        axis=0,
    )
    inverse_second = jnp.concatenate(
        [
            jnp.concatenate([second_cos, second_sin], axis=1),
            jnp.concatenate([-second_sin, second_cos], axis=1),
        ],
        axis=0,
    )
    return (first_both, twist_cos, twist_sin, forward_second, inverse_second)


def spectrum(series, tables):
    first_both, twist_cos, twist_sin, forward_second, inverse_second = tables
    channels, length = series.shape
    rows_k = twist_cos.shape[0]
    half = first_both.shape[1]
    second_len = twist_cos.shape[1]
    blocks = series.reshape(channels, half, length // half)
    part = jnp.einsum("ka,cab->ckb", first_both, blocks, precision=HIGHEST)
    part_re = part[:, :rows_k]
    part_im = part[:, rows_k:]
    turn_re = part_re * twist_cos + part_im * twist_sin
    turn_im = part_im * twist_cos - part_re * twist_sin
    turned = jnp.concatenate([turn_re, turn_im], axis=2)
    result = jnp.einsum("ckb,bm->ckm", turned, forward_second, precision=HIGHEST)
    return (result[:, :, :second_len], result[:, :, second_len:])


def signal_of(pair, tables):
    first_both, twist_cos, twist_sin, forward_second, inverse_second = tables
    spec_re, spec_im = pair
    channels = spec_re.shape[0]
    second_len = twist_cos.shape[1]
    total = twist_cos.shape[0] * second_len
    joined = jnp.concatenate([spec_re, spec_im], axis=2)
    back = jnp.einsum("ckm,mb->ckb", joined, inverse_second, precision=HIGHEST)
    back_re = back[:, :, :second_len]
    back_im = back[:, :, second_len:]
    turn_re = back_re * twist_cos - back_im * twist_sin
    turn_im = back_im * twist_cos + back_re * twist_sin
    turned = jnp.concatenate([turn_re, turn_im], axis=1)
    blocks = jnp.einsum("ka,ckb->cab", first_both, turned, precision=HIGHEST)
    return blocks.reshape(channels, -1) * (1.0 / total)


def product(left, right, conjugate):
    left_re, left_im = left
    right_re, right_im = right
    if conjugate:
        right_im = -right_im
    return (left_re * right_re - left_im * right_im, left_re * right_im + left_im * right_re)


def widen(array):
    return array.astype(jnp.float32)


def local(token_ids, field_offsets, embed_table, w_in, short_taps, filters, cotangent):
    tok_rows, width = cotangent.shape
    peers = lax.axis_size("tm")
    row_index = token_ids + field_offsets[None, :]
    embedded = jnp.sum(jnp.take(embed_table, row_index, axis=0).astype(jnp.float32), axis=1).astype(
        jnp.bfloat16
    )
    block = embedded
    proj = jnp.dot(
        block, lax.all_gather(w_in, "tm", axis=0, tiled=True), preferred_element_type=jnp.float32
    ).astype(jnp.bfloat16)
    before = shifted(proj[tok_rows - 2 :], "tm", 1)
    padded = jnp.concatenate([widen(before), widen(proj)], axis=0)
    mixed = (
        short_taps[0] * padded[2:]
        + short_taps[1] * padded[1 : tok_rows + 1]
        + short_taps[2] * padded[:tok_rows]
    ).astype(jnp.bfloat16)
    values = mixed[:, :width]
    first_gate = mixed[:, width : 2 * width]
    second_gate = mixed[:, 2 * width :]
    total = 2 * tok_rows * peers
    bits = total.bit_length() - 1
    first_len = 1 << (bits + 1) // 2
    second_len = total // first_len
    tables = build_tables(first_len, second_len, total)
    first_spec = spectrum(widen(filters[0]), tables)
    second_spec = spectrum(widen(filters[1]), tables)

    def split_time(series):
        return series.reshape(tok_rows, peers, -1)

    def channel_major(moved):
        return moved.reshape(moved.shape[0], -1).T

    def time_major(block):
        return block.T.reshape(block.shape[1], 1, block.shape[0])

    def to_channels(series):
        moved = lax.all_to_all(split_time(series), "tm", split_axis=1, concat_axis=0, tiled=True)
        return channel_major(moved)

    def to_time(block):
        moved = lax.all_to_all(time_major(block), "tm", split_axis=0, concat_axis=1, tiled=True)
        return moved.reshape(tok_rows, -1)

    value_spec = spectrum(widen(to_channels(values)), tables)
    first_conv = to_time(
        signal_of(product(value_spec, first_spec, False), tables).astype(jnp.bfloat16)
    )
    first_mix = (widen(first_gate) * widen(first_conv)).astype(jnp.bfloat16)
    mix_spec = spectrum(widen(to_channels(first_mix)), tables)
    second_conv = to_time(
        signal_of(product(mix_spec, second_spec, False), tables).astype(jnp.bfloat16)
    )
    mixer_out = (widen(second_gate) * widen(second_conv)).astype(jnp.bfloat16)
    upstream = widen(cotangent)
    grad_conv2 = (upstream * widen(second_gate)).astype(jnp.bfloat16)
    grad_gate2 = (upstream * widen(second_conv)).astype(jnp.bfloat16)
    grad_spec2 = spectrum(widen(to_channels(grad_conv2)), tables)
    grad_mix = to_time(
        signal_of(product(grad_spec2, second_spec, True), tables).astype(jnp.bfloat16)
    )
    filter_two = signal_of(product(grad_spec2, mix_spec, True), tables)
    grad_gate1 = (widen(grad_mix) * widen(first_conv)).astype(jnp.bfloat16)
    grad_conv1 = (widen(grad_mix) * widen(first_gate)).astype(jnp.bfloat16)
    grad_spec1 = spectrum(widen(to_channels(grad_conv1)), tables)
    grad_values = to_time(
        signal_of(product(grad_spec1, first_spec, True), tables).astype(jnp.bfloat16)
    )
    filter_one = signal_of(product(grad_spec1, value_spec, True), tables)
    filter_grads = jnp.stack([filter_one, filter_two], axis=0)
    grad_mixed = jnp.concatenate([grad_values, grad_gate1, grad_gate2], axis=1)
    after = shifted(grad_mixed[:2], "tm", -1)
    grad_wide = widen(grad_mixed)
    grad_padded = jnp.concatenate([grad_wide, widen(after)], axis=0)
    grad_proj = (
        short_taps[0] * grad_wide
        + short_taps[1] * grad_padded[1 : tok_rows + 1]
        + short_taps[2] * grad_padded[2:]
    ).astype(jnp.bfloat16)
    tap_terms = jnp.stack(
        [
            jnp.sum(grad_wide * padded[2:], axis=0),
            jnp.sum(grad_wide * padded[1 : tok_rows + 1], axis=0),
            jnp.sum(grad_wide * padded[:tok_rows], axis=0),
        ],
        axis=0,
    )
    tap_grads = lax.psum(tap_terms, "tm")
    block = embedded
    weight_grads = lax.psum_scatter(
        jnp.einsum("tr,tc->rc", block, grad_proj, preferred_element_type=jnp.float32),
        "tm",
        scatter_dimension=0,
        tiled=True,
    )
    return (mixer_out, weight_grads, tap_grads, filter_grads)


def solution(mesh):
    return jax.shard_map(
        local,
        mesh=mesh,
        in_specs=(
            P(("groups", "tm"), None),
            P("groups"),
            P(),
            P("tm", None),
            P(),
            P(None, "tm", None),
            P(("groups", "tm"), None),
        ),
        out_specs=(
            P(("groups", "tm"), None),
            P(("groups", "tm"), None),
            P("groups", None),
            P("groups", "tm", None),
        ),
        check_vma=False,
    )
```

profile of v0, /device:TPU:0, one launch (start us, length us, event | category | flops | bytes accessed | tf_op | source)
XLA Modules:
  0.0 535.3 jit_solution(3606033595169535217)
XLA Ops:
  19.8 55.1 %all-gather.2.cloned.1.call-done = bf16[1024,3072]{1,0:T(8,128)(2,1)} async-done(((bf16[64,3072]{1,0:T(8,128)(2,1)}), bf16[1024,3072]{1,0:T(8,128)(2,1)}) %all-gather.2.cloned.1.call-update) | async-done | bytes 6291472 | tf_op jit(solution)/shard_map/all_gather | solution.py:100
  93.4 7.6 %all-to-all-done.4 = bf16[128,16,64]{0,2,1:T(8,128)(2,1)} async-done(((bf16[128,16,64]{0,2,1:T(8,128)(2,1)}), bf16[128,16,64]{0,2,1:T(8,128)(2,1)}, u32[]{:S(2)}, u32[]{:S(2)}) %all-to-all-start.4) | async-done | bytes 262176 | tf_op jit(solution)/shard_map/all_to_all | solution.py:130
  107.2 6.7 %fusion.16 = f32[64,64,128]{2,1,0:T(8,128)S(1)} fusion(f32[128,128,1]{1,0,2:T(8,128)S(1)} %get-tuple-element.57, f32[64,64,64]{1,2,0:T(8,128)S(1)} %get-tuple-element.36, f32[64,64,64]{1,2,0:T(8,128)S(1)} %get-tuple-element.35), kind=kOutput, calls=%fused_computation.17 | convolution fusion | flops 805830656 | bytes 4259840 | tf_op jit(solution)/shard_map/ckb,bm->ckm/dot_general | solution.py:58
  113.9 7.2 %fusion.12 = f32[64,64,128]{2,1,0:T(8,128)S(1)} fusion(f32[128,128,1]{1,0,2:T(8,128)S(1)} %get-tuple-element.57, f32[64,64,64]{1,2,0:T(8,128)S(1)} %get-tuple-element.69, f32[64,64,64]{1,2,0:T(8,128)S(1)} %get-tuple-element.70), kind=kOutput, calls=%fused_computation.13 | convolution fusion | flops 805830656 | bytes 4259840 | tf_op jit(solution)/shard_map/ckb,bm->ckm/dot_general | solution.py:58
  148.7 6.8 %all-to-all-done.5 = bf16[16,2,4096]{2,1,0:T(2,128)(2,1)S(1)} async-done(((bf16[16,2,4096]{2,1,0:T(2,128)(2,1)}), bf16[16,2,4096]{2,1,0:T(2,128)(2,1)S(1)}, u32[]{:S(2)}, u32[]{:S(2)}) %all-to-all-start.5) | async-done | bytes 262176 | tf_op jit(solution)/shard_map/all_to_all | solution.py:134
  199.3 6.7 %fusion.20 = f32[64,64,128]{2,1,0:T(8,128)S(1)} fusion(f32[128,128,1]{1,0,2:T(8,128)S(1)} %get-tuple-element.57, f32[64,64,64]{1,2,0:T(8,128)S(1)} %get-tuple-element.34, f32[64,64,64]{1,2,0:T(8,128)S(1)} %get-tuple-element.33), kind=kOutput, calls=%fused_computation.21 | convolution fusion | flops 805830656 | bytes 4259840 | tf_op jit(solution)/shard_map/ckb,bm->ckm/dot_general | solution.py:58
  206.0 7.1 %fusion.4 = f32[64,64,128]{2,1,0:T(8,128)S(1)} fusion(f32[128,128,1]{1,0,2:T(8,128)S(1)} %get-tuple-element.57, f32[64,64,64]{1,2,0:T(8,128)S(1)} %get-tuple-element.65, f32[64,64,64]{1,2,0:T(8,128)S(1)} %get-tuple-element.66), kind=kOutput, calls=%fused_computation.5 | convolution fusion | flops 805830656 | bytes 4259840 | tf_op jit(solution)/shard_map/ckb,bm->ckm/dot_general | solution.py:58
  213.0 6.7 %fusion = f32[64,64,128]{2,1,0:T(8,128)S(1)} fusion(f32[128,128,1]{1,0,2:T(8,128)S(1)} %get-tuple-element.57, f32[64,64,64]{1,2,0:T(8,128)S(1)} %get-tuple-element.67, f32[64,64,64]{1,2,0:T(8,128)S(1)} %get-tuple-element.68), kind=kOutput, calls=%fused_computation.1 | convolution fusion | flops 805830656 | bytes 4259840 | tf_op jit(solution)/shard_map/ckb,bm->ckm/dot_general | solution.py:58
  227.0 8.3 %fusion.48 = f32[64,64,128]{1,2,0:T(8,128)S(1)} fusion(f32[128,128,1]{1,0,2:T(8,128)S(1)} %get-tuple-element.58, f32[64,64,64]{2,1,0:T(8,128)} %get-tuple-element.26, f32[64,64,64]{2,1,0:T(8,128)} %get-tuple-element.25), kind=kOutput, calls=%fused_computation.50 | convolution fusion | flops 805830656 | bytes 4259840 | tf_op jit(solution)/shard_map/ckm,mb->ckb/dot_general | solution.py:69
  235.3 6.2 %fusion.56 = f32[64,64,128]{1,2,0:T(8,128)S(1)} fusion(f32[128,128,1]{1,0,2:T(8,128)S(1)} %get-tuple-element.58, f32[64,64,64]{2,1,0:T(8,128)S(1)} %copy-done.9, f32[64,64,64]{2,1,0:T(8,128)S(1)} %copy-done.8), kind=kOutput, calls=%fused_computation.58 | convolution fusion | flops 805830656 | bytes 4259840 | tf_op jit(solution)/shard_map/ckm,mb->ckb/dot_general | solution.py:69
  241.5 6.2 %fusion.24 = f32[64,64,128]{1,2,0:T(8,128)S(1)} fusion(f32[128,128,1]{1,0,2:T(8,128)S(1)} %get-tuple-element.58, f32[64,64,64]{2,1,0:T(8,128)S(1)} %get-tuple-element.45, f32[64,64,64]{2,1,0:T(8,128)S(1)} %get-tuple-element.46), kind=kOutput, calls=%fused_computation.26 | convolution fusion | flops 805830656 | bytes 4259840 | tf_op jit(solution)/shard_map/ckm,mb->ckb/dot_general | solution.py:69
  252.3 6.6 %fusion.125 = bf16[64,32,64]{2,1,0:T(8,128)(2,1)} fusion(f32[128,32,1]{0,1,2:T(8,128)S(1)} %maximum_bitcast_fusion, f32[64,64,64]{1,2,0:T(8,128)S(1)} %get-tuple-element.59, f32[64,64,64]{1,2,0:T(8,128)S(1)} %get-tuple-element.60), kind=kOutput, calls=%fused_computation.150 | convolution fusion | flops 202113024 | bytes 2375680 | tf_op jit(solution)/shard_map/ka,ckb->cab/dot_general | solution.py:75
  267.6 16.1 %all_to_all.102 = bf16[16,2,4096]{2,1,0:T(2,128)(2,1)} all-to-all(bf16[16,2,4096]{2,1,0:T(2,128)(2,1)} %reshape.212), channel_id=1, replica_groups=mesh['groups'=2,'tm'=16] {'tm'}, dimensions={0} | all-to-all | bytes 524288 | tf_op jit(solution)/shard_map/all_to_all | solution.py:134
  302.5 8.0 %fusion.116 = bf16[64,32,64]{2,1,0:T(8,128)(2,1)S(1)} fusion(f32[128,32,1]{0,1,2:T(8,128)S(1)} %maximum_bitcast_fusion, f32[64,64,64]{1,2,0:T(8,128)} %get-tuple-element.61, f32[64,64,64]{1,2,0:T(8,128)} %get-tuple-element.62), kind=kOutput, calls=%fused_computation.147 | convolution fusion | flops 202113024 | bytes 2375680 | tf_op jit(solution)/shard_map/ka,ckb->cab/dot_general | solution.py:75
  316.5 6.4 %all-to-all-start.7 = ((bf16[16,2,4096]{2,1,0:T(2,128)(2,1)}), bf16[16,2,4096]{2,1,0:T(2,128)(2,1)}, u32[]{:S(2)}, u32[]{:S(2)}) async-start(bf16[16,2,4096]{2,1,0:T(2,128)(2,1)} %reshape.218), calls=%async_computation.7 | async-start | bytes 524288 | tf_op jit(solution)/shard_map/all_to_all | solution.py:134
  328.3 6.7 %fusion.8 = f32[64,64,128]{2,1,0:T(8,128)S(1)} fusion(f32[128,128,1]{1,0,2:T(8,128)S(1)} %get-tuple-element.57, f32[64,64,64]{1,2,0:T(8,128)S(1)} %get-tuple-element.38, f32[64,64,64]{1,2,0:T(8,128)S(1)} %get-tuple-element.37), kind=kOutput, calls=%fused_computation.9 | convolution fusion | flops 805830656 | bytes 4259840 | tf_op jit(solution)/shard_map/ckb,bm->ckm/dot_general | solution.py:58
  338.2 8.0 %fusion.64 = f32[64,64,128]{1,2,0:T(8,128)S(1)} fusion(f32[128,128,1]{1,0,2:T(8,128)S(1)} %get-tuple-element.58, f32[64,64,64]{2,1,0:T(8,128)} %get-tuple-element.24, f32[64,64,64]{2,1,0:T(8,128)S(1)} %get-tuple-element.23), kind=kOutput, calls=%fused_computation.66 | convolution fusion | flops 805830656 | bytes 4259840 | tf_op jit(solution)/shard_map/ckm,mb->ckb/dot_general | solution.py:69
  346.2 6.2 %fusion.32 = f32[64,64,128]{1,2,0:T(8,128)S(1)} fusion(f32[128,128,1]{1,0,2:T(8,128)S(1)} %get-tuple-element.58, f32[64,64,64]{2,1,0:T(8,128)S(1)} %get-tuple-element.47, f32[64,64,64]{2,1,0:T(8,128)S(1)} %get-tuple-element.48), kind=kOutput, calls=%fused_computation.34 | convolution fusion | flops 805830656 | bytes 4259840 | tf_op jit(solution)/shard_map/ckm,mb->ckb/dot_general | solution.py:69
  373.3 6.9 %all-to-all-done.3 = bf16[16,2,4096]{2,1,0:T(2,128)(2,1)S(1)} async-done(((bf16[16,2,4096]{2,1,0:T(2,128)(2,1)}), bf16[16,2,4096]{2,1,0:T(2,128)(2,1)S(1)}, u32[]{:S(2)}, u32[]{:S(2)}) %all-to-all-start.3) | async-done | bytes 262176 | tf_op jit(solution)/shard_map/all_to_all | solution.py:134
  386.6 6.4 %fusion.128 = f32[1024,3072]{1,0:T(8,128)} fusion(bf16[128,1024]{1,0:T(8,128)(2,1)S(1)} %copy-done.11, f32[128,3072]{1,0:T(8,128)S(1)} %get-tuple-element.50, f32[2,3072]{1,0:T(2,128)S(1)} %convert_element_type.300, f32[3072]{0:T(1024)S(1)} %bitcast.207, f32[3072]{0:T(1024)S(1)} %bitcast.209, f32[3072]{0:T(1024)S(1)} %bitcast.205), kind=kOutput, calls=%fused_computation.152 | convolution fusion | flops 808452096 | bytes 14479360 | tf_op jit(solution)/shard_map/tr,tc->rc/dot_general | solution.py:183
  394.7 7.4 %fusion.89 = f32[64,32,64]{2,1,0:T(8,128)S(1)} fusion(f32[128,32,1]{0,1,2:T(8,128)S(1)} %maximum_bitcast_fusion, f32[64,64,64]{1,2,0:T(8,128)} %get-tuple-element.10, f32[64,64,64]{1,2,0:T(8,128)S(1)} %copy-done.7), kind=kOutput, calls=%fused_computation.138 | convolution fusion | flops 201981952 | bytes 2637824 | tf_op jit(solution)/shard_map/ka,ckb->cab/dot_general | solution.py:75
  403.3 8.6 %fusion.83 = f32[64,32,64]{2,1,0:T(8,128)S(1)} fusion(f32[128,32,1]{0,1,2:T(8,128)S(1)} %maximum_bitcast_fusion, f32[64,64,64]{1,2,0:T(8,128)} %get-tuple-element.12, f32[64,64,64]{1,2,0:T(8,128)} %get-tuple-element.11), kind=kOutput, calls=%fused_computation.136 | convolution fusion | flops 201981952 | bytes 2637824 | tf_op jit(solution)/shard_map/ka,ckb->cab/dot_general | solution.py:75
  416.4 63.6 %psum.7 = f32[3,3072]{1,0:T(4,128)} all-reduce(f32[3,3072]{1,0:T(4,128)S(1)} %pad_maximum_fusion.8), channel_id=1, replica_groups=mesh['groups'=2,'tm'=16] {'tm'}, use_global_device_ids=true, to_apply=%region_5.6 | all-reduce | flops 9216 | bytes 73728 | tf_op jit(solution)/shard_map/psum | solution.py:180
  480.1 48.2 %reduce-scatter.2.cloned.1.call-done = f32[64,3072]{1,0:T(8,128)} async-done(((f32[1024,3072]{1,0:T(8,128)}), f32[64,3072]{1,0:T(8,128)}) %reduce-scatter.2.cloned.1.call-update) | async-done | bytes 786448 | tf_op jit(solution)/shard_map/reduce_scatter | solution.py:182
  (204 shorter events, 196.4 us)
Async XLA Ops:
  7.2 67.7 %all-gather.2.cloned.1.call-start = ((), (), s32[]{:S(2)}) async-start(), calls=%async_computation.9 | async-start | bytes 6684672 | tf_op jit(solution)/shard_map/all_gather | solution.py:100
  14.4 5.3 copy-start.36
  19.0 59.7 %copy-start.10 = (bf16[128,1024]{1,0:T(8,128)(2,1)}, bf16[128,1024]{1,0:T(8,128)(2,1)S(1)}, u32[]{:S(2)}) copy-start(bf16[128,1024]{1,0:T(8,128)(2,1)S(1)} %fusion.72) | copy-start | bytes 786436
  19.8 64.0 %copy-start.30 = (f32[1,3072]{1,0:T(1,128)}, f32[1,3072]{1,0:T(1,128)S(1)}, u32[]{:S(2)}) copy-start(f32[1,3072]{1,0:T(1,128)S(1)} %get-tuple-element.71) | copy-start | bytes 36868
  19.8 64.0 %copy-start.32 = (f32[1,3072]{1,0:T(1,128)}, f32[1,3072]{1,0:T(1,128)S(1)}, u32[]{:S(2)}) copy-start(f32[1,3072]{1,0:T(1,128)S(1)} %get-tuple-element.72) | copy-start | bytes 36868
  19.8 64.0 %copy-start.34 = (f32[1,3072]{1,0:T(1,128)}, f32[1,3072]{1,0:T(1,128)S(1)}, u32[]{:S(2)}) copy-start(f32[1,3072]{1,0:T(1,128)S(1)} %get-tuple-element.73) | copy-start | bytes 36868
  78.7 6.3 %copy-start.5 = (f32[128,3072]{1,0:T(8,128)}, f32[128,3072]{1,0:T(8,128)S(1)}, u32[]{:S(2)}) copy-start(f32[128,3072]{1,0:T(8,128)S(1)} %get-tuple-element.74) | copy-start | bytes 4718596
  78.7 6.2 %copy-start.25 = (bf16[128,1024]{1,0:T(8,128)(2,1)S(1)}, bf16[128,1024]{1,0:T(8,128)(2,1)}, u32[]{:S(2)}) copy-start(bf16[128,1024]{1,0:T(8,128)(2,1)} %param.13) | copy-start | bytes 786436
  79.6 4.2 collective-permute-start
  85.8 15.2 %all-to-all-start.4 = ((bf16[128,16,64]{0,2,1:T(8,128)(2,1)}), bf16[128,16,64]{0,2,1:T(8,128)(2,1)}, u32[]{:S(2)}, u32[]{:S(2)}) async-start(bf16[128,16,64]{0,2,1:T(8,128)(2,1)} %bitcast.31), calls=%async_computation.4 | async-start | bytes 524288 | tf_op jit(solution)/shard_map/all_to_all | solution.py:130
  142.0 13.5 %all-to-all-start.5 = ((bf16[16,2,4096]{2,1,0:T(2,128)(2,1)}), bf16[16,2,4096]{2,1,0:T(2,128)(2,1)S(1)}, u32[]{:S(2)}, u32[]{:S(2)}) async-start(bf16[16,2,4096]{2,1,0:T(2,128)(2,1)} %reshape.216), calls=%async_computation.5 | async-start | bytes 524288 | tf_op jit(solution)/shard_map/all_to_all | solution.py:134
  155.6 15.3 %all-to-all-start = ((bf16[128,16,64]{0,2,1:T(8,128)(2,1)}), bf16[128,16,64]{0,2,1:T(8,128)(2,1)}, u32[]{:S(2)}, u32[]{:S(2)}) async-start(bf16[128,16,64]{0,2,1:T(8,128)(2,1)} %bitcast.6), calls=%async_computation | async-start | bytes 524288 | tf_op jit(solution)/shard_map/all_to_all | solution.py:130
  170.9 17.3 %all-to-all-start.6 = ((bf16[128,16,64]{0,2,1:T(8,128)(2,1)}), bf16[128,16,64]{0,2,1:T(8,128)(2,1)}, u32[]{:S(2)}, u32[]{:S(2)}) async-start(bf16[128,16,64]{0,2,1:T(8,128)(2,1)} %bitcast.197), calls=%async_computation.6 | async-start | bytes 524288 | tf_op jit(solution)/shard_map/all_to_all | solution.py:130
  227.0 8.3 %copy-start.8 = (f32[64,64,64]{2,1,0:T(8,128)S(1)}, f32[64,64,64]{2,1,0:T(8,128)}, u32[]{:S(2)}) copy-start(f32[64,64,64]{2,1,0:T(8,128)} %get-tuple-element.21) | copy-start | bytes 3145732
  227.0 8.3 %copy-start.9 = (f32[64,64,64]{2,1,0:T(8,128)S(1)}, f32[64,64,64]{2,1,0:T(8,128)}, u32[]{:S(2)}) copy-start(f32[64,64,64]{2,1,0:T(8,128)} %get-tuple-element.22) | copy-start | bytes 3145732
  298.3 18.1 %all-to-all-start.2 = ((bf16[128,16,64]{0,2,1:T(8,128)(2,1)}), bf16[128,16,64]{0,2,1:T(8,128)(2,1)}, u32[]{:S(2)}, u32[]{:S(2)}) async-start(bf16[128,16,64]{0,2,1:T(8,128)(2,1)} %bitcast.20), calls=%async_computation.2 | async-start | bytes 524288 | tf_op jit(solution)/shard_map/all_to_all | solution.py:130
  316.5 47.8 %all-to-all-start.7 = ((bf16[16,2,4096]{2,1,0:T(2,128)(2,1)}), bf16[16,2,4096]{2,1,0:T(2,128)(2,1)}, u32[]{:S(2)}, u32[]{:S(2)}) async-start(bf16[16,2,4096]{2,1,0:T(2,128)(2,1)} %reshape.218), calls=%async_computation.7 | async-start | bytes 524288 | tf_op jit(solution)/shard_map/all_to_all | solution.py:134
  328.3 6.7 %copy-start.3 = (f32[64,64,128]{2,1,0:T(8,128)S(1)}, f32[64,64,128]{2,1,0:T(8,128)}, u32[]{:S(2)}) copy-start(f32[64,64,128]{2,1,0:T(8,128)} %copy-done.2) | copy-start | bytes 6291460
  364.2 16.0 %all-to-all-start.3 = ((bf16[16,2,4096]{2,1,0:T(2,128)(2,1)}), bf16[16,2,4096]{2,1,0:T(2,128)(2,1)S(1)}, u32[]{:S(2)}, u32[]{:S(2)}) async-start(bf16[16,2,4096]{2,1,0:T(2,128)(2,1)} %reshape.214), calls=%async_computation.3 | async-start | bytes 524288 | tf_op jit(solution)/shard_map/all_to_all | solution.py:134
  370.2 158.0 %reduce-scatter.2.cloned.1.call-start = ((), (), s32[]{:S(2)}) async-start(), calls=%async_computation.10 | async-start | bytes 13369344 | tf_op jit(solution)/shard_map/reduce_scatter | solution.py:182
  373.3 10.0 %copy-start.15 = (bf16[128,1024]{1,0:T(8,128)(2,1)}, bf16[128,1024]{1,0:T(8,128)(2,1)S(1)}, u32[]{:S(2)}) copy-start(bf16[128,1024]{1,0:T(8,128)(2,1)S(1)} %copy.256) | copy-start | bytes 786436
  383.3 9.8 %copy-start.17 = (bf16[128,1024]{1,0:T(8,128)(2,1)}, bf16[128,1024]{1,0:T(8,128)(2,1)S(1)}, u32[]{:S(2)}) copy-start(bf16[128,1024]{1,0:T(8,128)(2,1)S(1)} %get-tuple-element.53) | copy-start | bytes 786436
  383.5 3.1 collective-permute-start.1
  413.1 115.1 %copy-start.1 = (bf16[1024,1024]{1,0:T(8,128)(2,1)S(1)}, bf16[1024,1024]{1,0:T(8,128)(2,1)}, u32[]{:S(2)}) copy-start(bf16[1024,1024]{1,0:T(8,128)(2,1)} %param.9) | copy-start | bytes 6291460
  (24 other events, 58.8 us)
Sparse Core Ops, SparseCore 0:
  10.3 64.5 all-gather.1
  393.2 134.9 reduce-scatter.1
where the time goes:
time: 542 us; the launch traced here: 535 us
  matrix products  148 us (27%)
  waiting for transfers between devices  127 us (23%)
  blocking collectives  79.7 us (15%)
  local copies, waits for them, and re-layouts  74.7 us (14%)
  other arithmetic  51.6 us (10%)
  starting transfers between devices  39 us (7%)
  between operations  15.2 us (3%)
    psum x1, blocking collectives, local(): tap_grads = lax.psum(tap_terms, 'tm')  63.6 us
    all_gather x1, waiting for transfers between devices, local(): lax.all_gather(w_in, 'tm', axis=0, tiled=True)  55.1 us
    reduce_scatter x1, waiting for transfers between devices, local(): lax.psum_scatter(jnp.einsum('tr,tc->rc', block, grad_proj, preferred_elem...  48.2 us
    dot_general x6, matrix products, signal_of(): blocks = jnp.einsum('ka,ckb->cab', first_both, turned, precision=HIGHEST)  42.6 us
    dot_general x6, matrix products, signal_of(): back = jnp.einsum('ckm,mb->ckb', joined, inverse_second, precision=HIGHEST)  41 us
    dot_general x6, matrix products, spectrum(): jnp.einsum('ckb,bm->ckm', turned, forward_second, precision=HIGHEST)  40.9 us
    unnamed x94, local copies, waits for them, and re-layouts  25.1 us
    all_to_all x4, starting transfers between devices, to_channels(): lax.all_to_all(split_time(series), 'tm', split_axis=1, concat_axis=0, til...  19.6 us
  transfers between devices with their start and end apart: 11, of which 6 were waited for; matrix products, arithmetic and copies ran while one was open for 23% of the time, Pallas kernels for 0%

commit v1 on v0

--- a/solution.py
+++ b/solution.py
@@ -5,6 +5,28 @@
 from jax.sharding import PartitionSpec as P
 
 HIGHEST = lax.Precision.HIGHEST
+
+
+def cut_along(shard, dim, size):
+    before, after = (shard.shape[:dim], shard.shape[dim + 1 :])
+    return jnp.moveaxis(shard.reshape(*before, size, -1, *after), dim, 0)
+
+
+def in_order(pieces, dim):
+    lengths = list(pieces.shape[1:])
+    lengths[dim] *= pieces.shape[0]
+    return jnp.moveaxis(pieces, 0, dim).reshape(lengths)
+
+
+def exchange_in_pairs(x, axis, split_dim, concat_dim):
+    devices, index = (lax.axis_size(axis), lax.axis_index(axis))
+    blocks = cut_along(x, split_dim, devices)
+    outs = [blocks[index]]
+    for step in range(1, devices):
+        sent = blocks[index ^ step]
+        outs.append(lax.ppermute(sent, axis, [(i, i ^ step) for i in range(devices)]))
+    blocks = jnp.stack(outs)[index ^ jnp.arange(devices)]
+    return in_order(blocks, concat_dim)
 
 
 def shifted(value, axis, steps):
@@ -131,7 +153,7 @@
         return channel_major(moved)
 
     def to_time(block):
-        moved = lax.all_to_all(time_major(block), "tm", split_axis=0, concat_axis=1, tiled=True)
+        moved = exchange_in_pairs(time_major(block), "tm", 0, 1)
         return moved.reshape(tok_rows, -1)
 
     value_spec = spectrum(widen(to_channels(values)), tables)

time: 542 us -> 618 us (1.14)
  starting transfers between devices: 39 us -> 105 us
  local copies, waits for them, and re-layouts: 74.7 us -> 104 us
  blocking collectives: 79.7 us -> 64.9 us
  other arithmetic: 51.6 us -> 44.9 us
    ppermute x0 -> x60, starting transfers between devices: none -> 82.1 us  [exchange_in_pairs(): lax.ppermute(sent, axis, [(i, i ^ step) for i in range(devices)])]
    unnamed x94 -> x204, local copies, waits for them, and re-layouts: 25.1 us -> 53.3 us
    all_to_all x1 -> x0, blocking collectives: 16.1 us -> none  [to_time(): lax.all_to_all(time_major(block), 'tm', split_axis=0, concat_axis=1, tile...]
    all_to_all x3 -> x0, starting transfers between devices: 15.8 us -> none  [to_time(): lax.all_to_all(time_major(block), 'tm', split_axis=0, concat_axis=1, tile...]
    all_to_all x3 -> x0, waiting for transfers between devices: 13.8 us -> none  [to_time(): lax.all_to_all(time_major(block), 'tm', split_axis=0, concat_axis=1, tile...]
    ppermute x0 -> x60, waiting for transfers between devices: none -> 12.8 us  [exchange_in_pairs(): lax.ppermute(sent, axis, [(i, i ^ step) for i in range(devices)])]
    all_to_all x5 -> x0, local copies, waits for them, and re-layouts: 8.07 us -> none  [to_time(): lax.all_to_all(time_major(block), 'tm', split_axis=0, concat_axis=1, tile...]
    reshape x4 -> x0, other arithmetic: 7.99 us -> none  [time_major(): return block.T.reshape(block.shape[1], 1, block.shape[0])]
  transfers between devices with their start and end apart: 11 -> 68, of which waited for: 6 -> 11; matrix products, arithmetic and copies ran while one was open for 23% -> 26% of each run, Pallas kernels for 0% -> 0%
where the time goes in v1:
time: 618 us; the launch traced here: 610 us
  matrix products  150 us (24%)
  waiting for transfers between devices  125 us (20%)
  starting transfers between devices  105 us (17%)
  local copies, waits for them, and re-layouts  104 us (17%)
  blocking collectives  64.9 us (11%)
  other arithmetic  44.9 us (7%)
  between operations  15.7 us (3%)
    ppermute x60, starting transfers between devices, exchange_in_pairs(): lax.ppermute(sent, axis, [(i, i ^ step) for i in range(devices)])  82.1 us
    psum x1, blocking collectives, local(): tap_grads = lax.psum(tap_terms, 'tm')  64.9 us
    all_gather x1, waiting for transfers between devices, local(): lax.all_gather(w_in, 'tm', axis=0, tiled=True)  55.6 us
    unnamed x204, local copies, waits for them, and re-layouts  53.3 us
    reduce_scatter x1, waiting for transfers between devices, local(): lax.psum_scatter(jnp.einsum('tr,tc->rc', block, grad_proj, preferred_elem...  47.6 us
    dot_general x6, matrix products, signal_of(): blocks = jnp.einsum('ka,ckb->cab', first_both, turned, precision=HIGHEST)  44.3 us
    dot_general x6, matrix products, signal_of(): back = jnp.einsum('ckm,mb->ckb', joined, inverse_second, precision=HIGHEST)  41.3 us
    dot_general x6, matrix products, spectrum(): jnp.einsum('ckb,bm->ckm', turned, forward_second, precision=HIGHEST)  40.5 us
  transfers between devices with their start and end apart: 68, of which 11 were waited for; matrix products, arithmetic and copies ran while one was open for 26% of the time, Pallas kernels for 0%

profile of v1, /device:TPU:0, one launch (start us, length us, event | category | flops | bytes accessed | tf_op | source)
XLA Modules:
  0.0 609.9 jit_solution(3299184435155994247)
XLA Ops:
  19.3 55.6 %all-gather.2.cloned.1.call-done = bf16[1024,3072]{1,0:T(8,128)(2,1)} async-done(((bf16[64,3072]{1,0:T(8,128)(2,1)}), bf16[1024,3072]{1,0:T(8,128)(2,1)}) %all-gather.2.cloned.1.call-update) | async-done | bytes 6291472 | tf_op jit(solution)/shard_map/all_gather | solution.py:122
  94.6 6.5 %all-to-all-done.2 = bf16[128,16,64]{0,2,1:T(8,128)(2,1)} async-done(((bf16[128,16,64]{0,2,1:T(8,128)(2,1)}), bf16[128,16,64]{0,2,1:T(8,128)(2,1)}, u32[]{:S(2)}, u32[]{:S(2)}) %all-to-all-start.2) | async-done | bytes 262176 | tf_op jit(solution)/shard_map/all_to_all | solution.py:152
  112.0 6.7 %fusion.16 = f32[64,64,128]{2,1,0:T(8,128)S(1)} fusion(f32[128,128,1]{1,0,2:T(8,128)S(1)} %get-tuple-element.121, f32[64,64,64]{1,2,0:T(8,128)S(1)} %get-tuple-element.36, f32[64,64,64]{1,2,0:T(8,128)S(1)} %get-tuple-element.35), kind=kOutput, calls=%fused_computation.21 | convolution fusion | flops 805830656 | bytes 4259840 | tf_op jit(solution)/shard_map/ckb,bm->ckm/dot_general | solution.py:80
  118.6 7.0 %fusion.12 = f32[64,64,128]{2,1,0:T(8,128)S(1)} fusion(f32[128,128,1]{1,0,2:T(8,128)S(1)} %get-tuple-element.121, f32[64,64,64]{1,2,0:T(8,128)S(1)} %get-tuple-element.133, f32[64,64,64]{1,2,0:T(8,128)S(1)} %get-tuple-element.134), kind=kOutput, calls=%fused_computation.17 | convolution fusion | flops 805830656 | bytes 4259840 | tf_op jit(solution)/shard_map/ckb,bm->ckm/dot_general | solution.py:80
  127.0 6.2 %fusion.40 = f32[64,64,128]{1,2,0:T(8,128)S(1)} fusion(f32[128,128,1]{1,0,2:T(8,128)S(1)} %get-tuple-element.122, f32[64,64,64]{2,1,0:T(8,128)S(1)} %get-tuple-element.28, f32[64,64,64]{2,1,0:T(8,128)S(1)} %get-tuple-element.27), kind=kOutput, calls=%fused_computation.46 | convolution fusion | flops 805830656 | bytes 4259840 | tf_op jit(solution)/shard_map/ckm,mb->ckb/dot_general | solution.py:91
  134.1 6.0 fusion.119
  202.2 6.7 %fusion.20 = f32[64,64,128]{2,1,0:T(8,128)S(1)} fusion(f32[128,128,1]{1,0,2:T(8,128)S(1)} %get-tuple-element.121, f32[64,64,64]{1,2,0:T(8,128)S(1)} %get-tuple-element.34, f32[64,64,64]{1,2,0:T(8,128)S(1)} %get-tuple-element.33), kind=kOutput, calls=%fused_computation.25 | convolution fusion | flops 805830656 | bytes 4259840 | tf_op jit(solution)/shard_map/ckb,bm->ckm/dot_general | solution.py:80
  208.9 6.8 %fusion.4 = f32[64,64,128]{2,1,0:T(8,128)S(1)} fusion(f32[128,128,1]{1,0,2:T(8,128)S(1)} %get-tuple-element.121, f32[64,64,64]{1,2,0:T(8,128)S(1)} %get-tuple-element.129, f32[64,64,64]{1,2,0:T(8,128)S(1)} %get-tuple-element.130), kind=kOutput, calls=%fused_computation.9 | convolution fusion | flops 805830656 | bytes 4259840 | tf_op jit(solution)/shard_map/ckb,bm->ckm/dot_general | solution.py:80
  215.7 6.7 %fusion = f32[64,64,128]{2,1,0:T(8,128)S(1)} fusion(f32[128,128,1]{1,0,2:T(8,128)S(1)} %get-tuple-element.121, f32[64,64,64]{1,2,0:T(8,128)S(1)} %get-tuple-element.131, f32[64,64,64]{1,2,0:T(8,128)S(1)} %get-tuple-element.132), kind=kOutput, calls=%fused_computation.5 | convolution fusion | flops 805830656 | bytes 4259840 | tf_op jit(solution)/shard_map/ckb,bm->ckm/dot_general | solution.py:80
  229.5 8.3 %fusion.48 = f32[64,64,128]{1,2,0:T(8,128)S(1)} fusion(f32[128,128,1]{1,0,2:T(8,128)S(1)} %get-tuple-element.122, f32[64,64,64]{2,1,0:T(8,128)} %get-tuple-element.26, f32[64,64,64]{2,1,0:T(8,128)} %get-tuple-element.25), kind=kOutput, calls=%fused_computation.54 | convolution fusion | flops 805830656 | bytes 4259840 | tf_op jit(solution)/shard_map/ckm,mb->ckb/dot_general | solution.py:91
  237.8 6.2 %fusion.56 = f32[64,64,128]{1,2,0:T(8,128)S(1)} fusion(f32[128,128,1]{1,0,2:T(8,128)S(1)} %get-tuple-element.122, f32[64,64,64]{2,1,0:T(8,128)S(1)} %copy-done.9, f32[64,64,64]{2,1,0:T(8,128)S(1)} %copy-done.8), kind=kOutput, calls=%fused_computation.62 | convolution fusion | flops 805830656 | bytes 4259840 | tf_op jit(solution)/shard_map/ckm,mb->ckb/dot_general | solution.py:91
  244.1 6.2 %fusion.24 = f32[64,64,128]{1,2,0:T(8,128)S(1)} fusion(f32[128,128,1]{1,0,2:T(8,128)S(1)} %get-tuple-element.122, f32[64,64,64]{2,1,0:T(8,128)S(1)} %get-tuple-element.45, f32[64,64,64]{2,1,0:T(8,128)S(1)} %get-tuple-element.46), kind=kOutput, calls=%fused_computation.30 | convolution fusion | flops 805830656 | bytes 4259840 | tf_op jit(solution)/shard_map/ckm,mb->ckb/dot_general | solution.py:91
  255.0 6.6 %fusion.125 = bf16[64,32,64]{2,1,0:T(8,128)(2,1)} fusion(f32[128,32,1]{0,1,2:T(8,128)S(1)} %maximum_bitcast_fusion, f32[64,64,64]{1,2,0:T(8,128)S(1)} %get-tuple-element.123, f32[64,64,64]{1,2,0:T(8,128)S(1)} %get-tuple-element.124), kind=kOutput, calls=%fused_computation.154 | convolution fusion | flops 202113024 | bytes 2375680 | tf_op jit(solution)/shard_map/ka,ckb->cab/dot_general | solution.py:97
  273.5 8.8 %fusion.116 = bf16[64,32,64]{2,1,0:T(8,128)(2,1)} fusion(f32[128,32,1]{0,1,2:T(8,128)S(1)} %maximum_bitcast_fusion, f32[64,64,64]{1,2,0:T(8,128)} %get-tuple-element.125, f32[64,64,64]{1,2,0:T(8,128)} %get-tuple-element.126), kind=kOutput, calls=%fused_computation.151 | convolution fusion | flops 202113024 | bytes 2375680 | tf_op jit(solution)/shard_map/ka,ckb->cab/dot_general | solution.py:97
  346.3 5.8 all-to-all-start.1
  394.5 6.7 %fusion.8 = f32[64,64,128]{2,1,0:T(8,128)S(1)} fusion(f32[128,128,1]{1,0,2:T(8,128)S(1)} %get-tuple-element.121, f32[64,64,64]{1,2,0:T(8,128)S(1)} %get-tuple-element.38, f32[64,64,64]{1,2,0:T(8,128)S(1)} %get-tuple-element.37), kind=kOutput, calls=%fused_computation.13 | convolution fusion | flops 805830656 | bytes 4259840 | tf_op jit(solution)/shard_map/ckb,bm->ckm/dot_general | solution.py:80
  404.3 8.2 %fusion.64 = f32[64,64,128]{1,2,0:T(8,128)S(1)} fusion(f32[128,128,1]{1,0,2:T(8,128)S(1)} %get-tuple-element.122, f32[64,64,64]{2,1,0:T(8,128)} %get-tuple-element.24, f32[64,64,64]{2,1,0:T(8,128)S(1)} %get-tuple-element.23), kind=kOutput, calls=%fused_computation.70 | convolution fusion | flops 805830656 | bytes 4259840 | tf_op jit(solution)/shard_map/ckm,mb->ckb/dot_general | solution.py:91
  412.5 6.2 %fusion.32 = f32[64,64,128]{1,2,0:T(8,128)S(1)} fusion(f32[128,128,1]{1,0,2:T(8,128)S(1)} %get-tuple-element.122, f32[64,64,64]{2,1,0:T(8,128)S(1)} %get-tuple-element.47, f32[64,64,64]{2,1,0:T(8,128)S(1)} %get-tuple-element.48), kind=kOutput, calls=%fused_computation.38 | convolution fusion | flops 805830656 | bytes 4259840 | tf_op jit(solution)/shard_map/ckm,mb->ckb/dot_general | solution.py:91
  422.0 6.8 %fusion.122 = bf16[64,32,64]{2,1,0:T(8,128)(2,1)} fusion(f32[128,32,1]{0,1,2:T(8,128)S(1)} %maximum_bitcast_fusion, f32[64,64,64]{1,2,0:T(8,128)S(1)} %get-tuple-element.127, f32[64,64,64]{1,2,0:T(8,128)S(1)} %get-tuple-element.128), kind=kOutput, calls=%fused_computation.153 | convolution fusion | flops 202113024 | bytes 2375680 | tf_op jit(solution)/shard_map/ka,ckb->cab/dot_general | solution.py:97
  460.5 6.4 %fusion.128 = f32[1024,3072]{1,0:T(8,128)} fusion(bf16[128,1024]{1,0:T(8,128)(2,1)S(1)} %copy-done.11, f32[128,3072]{1,0:T(8,128)S(1)} %get-tuple-element.50, f32[2,3072]{1,0:T(2,128)S(1)} %convert_element_type.288, f32[3072]{0:T(1024)S(1)} %bitcast.631, f32[3072]{0:T(1024)S(1)} %bitcast.633, f32[3072]{0:T(1024)S(1)} %bitcast.629), kind=kOutput, calls=%fused_computation.156 | convolution fusion | flops 808452096 | bytes 14479360 | tf_op jit(solution)/shard_map/tr,tc->rc/dot_general | solution.py:205
  468.6 7.4 %fusion.89 = f32[64,32,64]{2,1,0:T(8,128)S(1)} fusion(f32[128,32,1]{0,1,2:T(8,128)S(1)} %maximum_bitcast_fusion, f32[64,64,64]{1,2,0:T(8,128)} %get-tuple-element.10, f32[64,64,64]{1,2,0:T(8,128)S(1)} %copy-done.7), kind=kOutput, calls=%fused_computation.142 | convolution fusion | flops 201981952 | bytes 2637824 | tf_op jit(solution)/shard_map/ka,ckb->cab/dot_general | solution.py:97
  477.2 8.6 %fusion.83 = f32[64,32,64]{2,1,0:T(8,128)S(1)} fusion(f32[128,32,1]{0,1,2:T(8,128)S(1)} %maximum_bitcast_fusion, f32[64,64,64]{1,2,0:T(8,128)} %get-tuple-element.12, f32[64,64,64]{1,2,0:T(8,128)} %get-tuple-element.11), kind=kOutput, calls=%fused_computation.140 | convolution fusion | flops 201981952 | bytes 2637824 | tf_op jit(solution)/shard_map/ka,ckb->cab/dot_general | solution.py:97
  490.3 64.9 %psum.7 = f32[3,3072]{1,0:T(4,128)} all-reduce(f32[3,3072]{1,0:T(4,128)S(1)} %pad_maximum_fusion.8), channel_id=1, replica_groups=mesh['groups'=2,'tm'=16] {'tm'}, use_global_device_ids=true, to_apply=%region_5.6 | all-reduce | flops 9216 | bytes 73728 | tf_op jit(solution)/shard_map/psum | solution.py:202
  555.3 47.6 %reduce-scatter.2.cloned.1.call-done = f32[64,3072]{1,0:T(8,128)} async-done(((f32[1024,3072]{1,0:T(8,128)}), f32[64,3072]{1,0:T(8,128)}) %reduce-scatter.2.cloned.1.call-update) | async-done | bytes 786448 | tf_op jit(solution)/shard_map/reduce_scatter | solution.py:204
  (428 shorter events, 281.2 us)
Async XLA Ops:
  7.2 67.7 %all-gather.2.cloned.1.call-start = ((), (), s32[]{:S(2)}) async-start(), calls=%async_computation.5 | async-start | bytes 6684672 | tf_op jit(solution)/shard_map/all_gather | solution.py:122
  86.7 14.4 %all-to-all-start.2 = ((bf16[128,16,64]{0,2,1:T(8,128)(2,1)}), bf16[128,16,64]{0,2,1:T(8,128)(2,1)}, u32[]{:S(2)}, u32[]{:S(2)}) async-start(bf16[128,16,64]{0,2,1:T(8,128)(2,1)} %bitcast.94), calls=%async_computation.2 | async-start | bytes 524288 | tf_op jit(solution)/shard_map/all_to_all | solution.py:152
  101.1 74.3 %all-to-all-start = ((bf16[128,16,64]{0,2,1:T(8,128)(2,1)}), bf16[128,16,64]{0,2,1:T(8,128)(2,1)}, u32[]{:S(2)}, u32[]{:S(2)}) async-start(bf16[128,16,64]{0,2,1:T(8,128)(2,1)} %bitcast.6), calls=%async_computation | async-start | bytes 524288 | tf_op jit(solution)/shard_map/all_to_all | solution.py:152
  175.4 15.5 %all-to-all-start.3 = ((bf16[128,16,64]{0,2,1:T(8,128)(2,1)}), bf16[128,16,64]{0,2,1:T(8,128)(2,1)}, u32[]{:S(2)}, u32[]{:S(2)}) async-start(bf16[128,16,64]{0,2,1:T(8,128)(2,1)} %bitcast.623), calls=%async_computation.3 | async-start | bytes 524288 | tf_op jit(solution)/shard_map/all_to_all | solution.py:152
  269.2 33.7 %collective-permute-start.1 = (bf16[128,1,64]{0,2,1:T(8,128)(2,1)}, bf16[128,1,64]{0,2,1:T(8,128)(2,1)}, u32[]{:S(2)}, u32[]{:S(2)}) collective-permute-start(bf16[128,1,64]{0,2,1:T(8,128)(2,1)} %bitcast.603), channel_id=1, source_target_pairs={{0,1},{1,0},{2,3},{3,2},{4,5},{5,4},{6,7},{7,6},{8,9},{9,8},{10,11... | collective-permute-start | bytes 49160 | tf_op jit(solution)/shard_map/ppermute | solution.py:27
  269.4 37.4 %collective-permute-start.2 = (bf16[128,1,64]{0,2,1:T(8,128)(2,1)}, bf16[128,1,64]{0,2,1:T(8,128)(2,1)}, u32[]{:S(2)}, u32[]{:S(2)}) collective-permute-start(bf16[128,1,64]{0,2,1:T(8,128)(2,1)} %bitcast.602), channel_id=1, source_target_pairs={{0,2},{1,3},{2,0},{3,1},{4,6},{5,7},{6,4},{7,5},{8,10},{9,11},{10,... | collective-permute-start | bytes 49160 | tf_op jit(solution)/shard_map/ppermute | solution.py:27
  271.1 37.0 %collective-permute-start.3 = (bf16[128,1,64]{0,2,1:T(8,128)(2,1)}, bf16[128,1,64]{0,2,1:T(8,128)(2,1)}, u32[]{:S(2)}, u32[]{:S(2)}) collective-permute-start(bf16[128,1,64]{0,2,1:T(8,128)(2,1)} %bitcast.601), channel_id=1, source_target_pairs={{0,3},{1,2},{2,1},{3,0},{4,7},{5,6},{6,5},{7,4},{8,11},{9,10},{10,... | collective-permute-start | bytes 49160 | tf_op jit(solution)/shard_map/ppermute | solution.py:27
  271.1 41.0 %collective-permute-start.4 = (bf16[128,1,64]{0,2,1:T(8,128)(2,1)}, bf16[128,1,64]{0,2,1:T(8,128)(2,1)}, u32[]{:S(2)}, u32[]{:S(2)}) collective-permute-start(bf16[128,1,64]{0,2,1:T(8,128)(2,1)} %bitcast.600), channel_id=1, source_target_pairs={{0,4},{1,5},{2,6},{3,7},{4,0},{5,1},{6,2},{7,3},{8,12},{9,13},{10,... | collective-permute-start | bytes 49160 | tf_op jit(solution)/shard_map/ppermute | solution.py:27
  272.8 40.7 %collective-permute-start.5 = (bf16[128,1,64]{0,2,1:T(8,128)(2,1)}, bf16[128,1,64]{0,2,1:T(8,128)(2,1)}, u32[]{:S(2)}, u32[]{:S(2)}) collective-permute-start(bf16[128,1,64]{0,2,1:T(8,128)(2,1)} %bitcast.599), channel_id=1, source_target_pairs={{0,5},{1,4},{2,7},{3,6},{4,1},{5,0},{6,3},{7,2},{8,13},{9,12},{10,... | collective-permute-start | bytes 49160 | tf_op jit(solution)/shard_map/ppermute | solution.py:27
  302.9 15.5 %collective-permute-start.6 = (bf16[128,1,64]{0,2,1:T(8,128)(2,1)S(1)}, bf16[128,1,64]{0,2,1:T(8,128)(2,1)S(1)}, u32[]{:S(2)}, u32[]{:S(2)}) collective-permute-start(bf16[128,1,64]{0,2,1:T(8,128)(2,1)S(1)} %bitcast.672), channel_id=1, source_target_pairs={{0,6},{1,7},{2,4},{3,5},{4,2},{5,3},{6,0},{7,1},{8,14},{9,15},{10,... | collective-permute-start | bytes 49160 | tf_op jit(solution)/shard_map/ppermute | solution.py:27
  306.8 12.1 %collective-permute-start.7 = (bf16[128,1,64]{0,2,1:T(8,128)(2,1)S(1)}, bf16[128,1,64]{0,2,1:T(8,128)(2,1)S(1)}, u32[]{:S(2)}, u32[]{:S(2)}) collective-permute-start(bf16[128,1,64]{0,2,1:T(8,128)(2,1)S(1)} %bitcast.667), channel_id=1, source_target_pairs={{0,7},{1,6},{2,5},{3,4},{4,3},{5,2},{6,1},{7,0},{8,15},{9,14},{10,... | collective-permute-start | bytes 49160 | tf_op jit(solution)/shard_map/ppermute | solution.py:27
  308.2 14.9 %collective-permute-start.8 = (bf16[128,1,64]{0,2,1:T(8,128)(2,1)S(1)}, bf16[128,1,64]{0,2,1:T(8,128)(2,1)S(1)}, u32[]{:S(2)}, u32[]{:S(2)}) collective-permute-start(bf16[128,1,64]{0,2,1:T(8,128)(2,1)S(1)} %bitcast.664), channel_id=1, source_target_pairs={{0,8},{1,9},{2,10},{3,11},{4,12},{5,13},{6,14},{7,15},{8,0},{9,1},... | collective-permute-start | bytes 49160 | tf_op jit(solution)/shard_map/ppermute | solution.py:27
  313.5 15.3 %collective-permute-start.10 = (bf16[128,1,64]{0,2,1:T(8,128)(2,1)S(1)}, bf16[128,1,64]{0,2,1:T(8,128)(2,1)S(1)}, u32[]{:S(2)}, u32[]{:S(2)}) collective-permute-start(bf16[128,1,64]{0,2,1:T(8,128)(2,1)S(1)} %bitcast.657), channel_id=1, source_target_pairs={{0,10},{1,11},{2,8},{3,9},{4,14},{5,15},{6,12},{7,13},{8,2},{9,3},... | collective-permute-start | bytes 49160 | tf_op jit(solution)/shard_map/ppermute | solution.py:27
  329.4 23.0 %collective-permute-start.46 = (bf16[128,1,64]{0,2,1:T(8,128)(2,1)}, bf16[128,1,64]{0,2,1:T(8,128)(2,1)}, u32[]{:S(2)}, u32[]{:S(2)}) collective-permute-start(bf16[128,1,64]{0,2,1:T(8,128)(2,1)} %bitcast.558), channel_id=1, source_target_pairs={{0,1},{1,0},{2,3},{3,2},{4,5},{5,4},{6,7},{7,6},{8,9},{9,8},{10,11... | collective-permute-start | bytes 49160 | tf_op jit(solution)/shard_map/ppermute | solution.py:27
  330.5 26.1 %collective-permute-start.47 = (bf16[128,1,64]{0,2,1:T(8,128)(2,1)}, bf16[128,1,64]{0,2,1:T(8,128)(2,1)}, u32[]{:S(2)}, u32[]{:S(2)}) collective-permute-start(bf16[128,1,64]{0,2,1:T(8,128)(2,1)} %bitcast.557), channel_id=1, source_target_pairs={{0,2},{1,3},{2,0},{3,1},{4,6},{5,7},{6,4},{7,5},{8,10},{9,11},{10,... | collective-permute-start | bytes 49160 | tf_op jit(solution)/shard_map/ppermute | solution.py:27
  332.7 25.2 %collective-permute-start.48 = (bf16[128,1,64]{0,2,1:T(8,128)(2,1)}, bf16[128,1,64]{0,2,1:T(8,128)(2,1)}, u32[]{:S(2)}, u32[]{:S(2)}) collective-permute-start(bf16[128,1,64]{0,2,1:T(8,128)(2,1)} %bitcast.556), channel_id=1, source_target_pairs={{0,3},{1,2},{2,1},{3,0},{4,7},{5,6},{6,5},{7,4},{8,11},{9,10},{10,... | collective-permute-start | bytes 49160 | tf_op jit(solution)/shard_map/ppermute | solution.py:27
  333.3 28.3 %collective-permute-start.49 = (bf16[128,1,64]{0,2,1:T(8,128)(2,1)}, bf16[128,1,64]{0,2,1:T(8,128)(2,1)}, u32[]{:S(2)}, u32[]{:S(2)}) collective-permute-start(bf16[128,1,64]{0,2,1:T(8,128)(2,1)} %bitcast.555), channel_id=1, source_target_pairs={{0,4},{1,5},{2,6},{3,7},{4,0},{5,1},{6,2},{7,3},{8,12},{9,13},{10,... | collective-permute-start | bytes 49160 | tf_op jit(solution)/shard_map/ppermute | solution.py:27
  334.7 28.5 %collective-permute-start.50 = (bf16[128,1,64]{0,2,1:T(8,128)(2,1)}, bf16[128,1,64]{0,2,1:T(8,128)(2,1)}, u32[]{:S(2)}, u32[]{:S(2)}) collective-permute-start(bf16[128,1,64]{0,2,1:T(8,128)(2,1)} %bitcast.554), channel_id=1, source_target_pairs={{0,5},{1,4},{2,7},{3,6},{4,1},{5,0},{6,3},{7,2},{8,13},{9,12},{10,... | collective-permute-start | bytes 49160 | tf_op jit(solution)/shard_map/ppermute | solution.py:27
  346.3 40.7 %all-to-all-start.1 = ((bf16[128,16,64]{0,2,1:T(8,128)(2,1)}), bf16[128,16,64]{0,2,1:T(8,128)(2,1)}, u32[]{:S(2)}, u32[]{:S(2)}) async-start(bf16[128,16,64]{0,2,1:T(8,128)(2,1)} %bitcast.52), calls=%async_computation.1 | async-start | bytes 524288 | tf_op jit(solution)/shard_map/all_to_all | solution.py:152
  352.2 250.7 %reduce-scatter.2.cloned.1.call-start = ((), (), s32[]{:S(2)}) async-start(), calls=%async_computation.6 | async-start | bytes 13369344 | tf_op jit(solution)/shard_map/reduce_scatter | solution.py:204
  352.4 15.6 %collective-permute-start.51 = (bf16[128,1,64]{0,2,1:T(8,128)(2,1)}, bf16[128,1,64]{0,2,1:T(8,128)(2,1)S(1)}, u32[]{:S(2)}, u32[]{:S(2)}) collective-permute-start(bf16[128,1,64]{0,2,1:T(8,128)(2,1)} %bitcast.646), channel_id=1, source_target_pairs={{0,6},{1,7},{2,4},{3,5},{4,2},{5,3},{6,0},{7,1},{8,14},{9,15},{10,... | collective-permute-start | bytes 49160 | tf_op jit(solution)/shard_map/ppermute | solution.py:27
  356.6 12.1 %collective-permute-start.52 = (bf16[128,1,64]{0,2,1:T(8,128)(2,1)}, bf16[128,1,64]{0,2,1:T(8,128)(2,1)S(1)}, u32[]{:S(2)}, u32[]{:S(2)}) collective-permute-start(bf16[128,1,64]{0,2,1:T(8,128)(2,1)} %bitcast.645), channel_id=1, source_target_pairs={{0,7},{1,6},{2,5},{3,4},{4,3},{5,2},{6,1},{7,0},{8,15},{9,14},{10,... | collective-permute-start | bytes 49160 | tf_op jit(solution)/shard_map/ppermute | solution.py:27
  357.9 14.7 %collective-permute-start.53 = (bf16[128,1,64]{0,2,1:T(8,128)(2,1)}, bf16[128,1,64]{0,2,1:T(8,128)(2,1)S(1)}, u32[]{:S(2)}, u32[]{:S(2)}) collective-permute-start(bf16[128,1,64]{0,2,1:T(8,128)(2,1)} %bitcast.644), channel_id=1, source_target_pairs={{0,8},{1,9},{2,10},{3,11},{4,12},{5,13},{6,14},{7,15},{8,0},{9,1},... | collective-permute-start | bytes 49160 | tf_op jit(solution)/shard_map/ppermute | solution.py:27
  363.2 15.3 %collective-permute-start.55 = (bf16[128,1,64]{0,2,1:T(8,128)(2,1)}, bf16[128,1,64]{0,2,1:T(8,128)(2,1)S(1)}, u32[]{:S(2)}, u32[]{:S(2)}) collective-permute-start(bf16[128,1,64]{0,2,1:T(8,128)(2,1)} %bitcast.642), channel_id=1, source_target_pairs={{0,10},{1,11},{2,8},{3,9},{4,14},{5,15},{6,12},{7,13},{8,2},{9,3},... | collective-permute-start | bytes 49160 | tf_op jit(solution)/shard_map/ppermute | solution.py:27
  (82 other events, 927.6 us)
Sparse Core Ops, SparseCore 0:
  10.3 64.5 all-gather.1
  467.1 135.6 reduce-scatter.1
